TPU v7x, 32 devices: a whole 2x2x4 slice. The times are simulated.
32 devices in a mesh: row: 8 (over z, core), col: 4 (over y, x).
Axes of the slice: x: 2, y: 2, z: 4, core: 2. Of those that a mesh axis runs over, the one named last changes fastest.
Arguments:
- atom_feats: bfloat16 [5120, 128], P(('row', 'col')), may hold values from -6 to 6
- atom_bias: float32 [4, 5120, 128], P(None, ('row', 'col')), may hold values from -5 to 360
- atom_counts: int32 [1280], replicated, may hold values from 1 to 24, 5120 in all
- valid_tokens: int32 [1], replicated, may hold values from 640 to 1280
- pair_in: bfloat16 [256, 1280, 128], P('row', 'col'), may hold values from -6 to 6
- atom_gain: float32 [128], replicated, may hold values from 0.5 to 1.5
- atom_proj: bfloat16 [128, 512], replicated, may hold values from -0.5 to 0.5
- atom_out: bfloat16 [128, 128], replicated, may hold values from -4 to 4
- atom_pool: bfloat16 [128, 384], replicated, may hold values from -0.5 to 0.5
- single_to_pair: bfloat16 [384, 256], replicated, may hold values from -0.3125 to 0.3125
- pair_gains: float32 [3, 128], replicated, may hold values from 0.5 to 1.5
- trans_in: bfloat16 [128, 1024], replicated, may hold values from -0.5 to 0.5
- trans_out: bfloat16 [512, 128], replicated, may hold values from -0.25 to 0.25
- tri_in: bfloat16 [128, 512], replicated, may hold values from -0.5 to 0.5
- tri_out: bfloat16 [128, 128], replicated, may hold values from -0.5 to 0.5
Outputs:
- single: bfloat16 [1280, 384], P('col')
- update: bfloat16 [256, 256, 128], P('row', 'col')
Inputs may be any that keep to these rules, and one draw needn't show every extreme that they name: `atom_counts`: the counts sum to 5120; some token has exactly 24 atoms.
All inputs are finite; a program needn't handle non-finite values.
Results may differ from a plain program's by a relative error of at most 0.0091.
Values may be sent and summed in bfloat16 or wider, within the bound.
No kernel may reach another device: no remote copies, remote signals or barrier semaphores. Data moves between devices by JAX's collectives and lax.ppermute only.
A program may use at most 128 MiB of HBM per device.

v0:
```python
import jax
import jax.numpy as jnp
from jax import lax
from jax.sharding import PartitionSpec as P

QBLOCK = 32
KEYS = 128
RIM = 48
EPS = 1e-05


def padded(shard, sides, width):
    for axis, dim in sides:
        size, length = (lax.axis_size(axis), shard.shape[dim])
        up = [(i, (i + 1) % size) for i in range(size - 1)]
        down = [(j, i) for i, j in up]
        last = lax.slice_in_dim(shard, length - width, length, axis=dim)
        initial = lax.slice_in_dim(shard, 0, width, axis=dim)
        before = lax.ppermute(last, axis, up)
        after = lax.ppermute(initial, axis, down)
        shard = jnp.concatenate([before, shard, after], axis=dim)
    return shard


def normalize(values, gain_row):
    values = values.astype(jnp.float32)
    average = jnp.mean(values, axis=-1, keepdims=True)
    centered = values - average
    variance = jnp.mean(centered * centered, axis=-1, keepdims=True)
    return centered * lax.rsqrt(variance + EPS) * gain_row


def attend(queries, key_vals, gating, atom_bias, first_atom, total_atoms):
    atom_rows, atom_width = queries.shape
    blocks = atom_rows // QBLOCK
    head_count = atom_bias.shape[0]
    head_size = atom_width // head_count
    windowed = jnp.stack(
        [key_vals[QBLOCK * block_id : QBLOCK * block_id + KEYS] for block_id in range(blocks)]
    )
    position = (
        first_atom
        - RIM
        + (jnp.arange(blocks, dtype=jnp.int32) * QBLOCK)[:, None]
        + jnp.arange(KEYS, dtype=jnp.int32)[None, :]
    )
    in_range = (position >= 0) & (position < total_atoms)
    query_heads = queries.reshape(blocks, QBLOCK, head_count, head_size)
    key_heads = windowed[:, :, :atom_width].reshape(blocks, KEYS, head_count, head_size)
    value_heads = windowed[:, :, atom_width:].reshape(blocks, KEYS, head_count, head_size)
    scores = jnp.einsum(
        "bqhd,bkhd->bhqk", query_heads, key_heads, preferred_element_type=jnp.float32
    ) * head_size ** (-0.5)
    bias_rows = atom_bias.reshape(head_count, blocks, QBLOCK, KEYS).transpose(1, 0, 2, 3)
    scores = jnp.where(in_range[:, None, None, :], scores + bias_rows, -1e30)
    row_max = jnp.max(scores, axis=-1, keepdims=True)
    exponent = jnp.exp(scores - row_max)
    weights = (exponent / jnp.sum(exponent, axis=-1, keepdims=True)).astype(jnp.bfloat16)
    blended = jnp.einsum(
        "bhqk,bkhd->bqhd", weights, value_heads, preferred_element_type=jnp.float32
    )
    return (blended.reshape(atom_rows, atom_width) * gating).astype(jnp.bfloat16)


def body(
    atom_feats,
    atom_bias,
    atom_counts,
    valid_tokens,
    pair_in,
    atom_gain,
    atom_proj,
    atom_out,
    atom_pool,
    single_to_pair,
    pair_gains,
    trans_in,
    trans_out,
    tri_in,
    tri_out,
):
    atom_rows, atom_width = atom_feats.shape
    position = lax.axis_index(("row", "col"))
    total_atoms = atom_rows * lax.axis_size(("row", "col"))
    first_atom = position * atom_rows
    normed = normalize(atom_feats, atom_gain).astype(jnp.bfloat16)
    projected = jnp.dot(normed, atom_proj, preferred_element_type=jnp.float32)
    queries = projected[:, :atom_width].astype(jnp.bfloat16)
    gating = jax.nn.sigmoid(projected[:, 3 * atom_width :])
    key_vals = projected[:, atom_width : 3 * atom_width].astype(jnp.bfloat16)
    key_vals = padded(key_vals, ((("row", "col"), 0),), RIM)
    gated = attend(queries, key_vals, gating, atom_bias, first_atom, total_atoms)
    updated = (
        atom_feats.astype(jnp.float32)
        + jnp.dot(gated, atom_out, preferred_element_type=jnp.float32)
    ).astype(jnp.bfloat16)
    hidden = jax.nn.relu(jnp.dot(updated, atom_pool, preferred_element_type=jnp.float32))
    tokens = atom_counts.shape[0]
    token_ends = jnp.cumsum(atom_counts)
    starts = token_ends - atom_counts
    atom_index = first_atom + jnp.arange(atom_rows, dtype=jnp.int32)
    owners = jnp.sum((starts[None, :] <= atom_index[:, None]).astype(jnp.int32), axis=1) - 1
    first_token = owners[0]
    offsets = owners - first_token
    onehot = (offsets[None, :] == jnp.arange(atom_rows, dtype=jnp.int32)[:, None]).astype(
        jnp.float32
    )
    window = jnp.dot(onehot, hidden, precision=lax.Precision.HIGHEST)
    table_sums = jnp.zeros((tokens + atom_rows, hidden.shape[1]), jnp.float32)
    table_sums = lax.dynamic_update_slice_in_dim(table_sums, window, first_token, 0)[:tokens]
    count_float = atom_counts.astype(jnp.float32)
    totals = lax.psum(table_sums, ("row", "col"))
    single_all = (totals / count_float[:, None]).astype(jnp.bfloat16)
    row_dev, tok_col, channels = pair_in.shape
    col_place = lax.axis_index("col")
    row_place = lax.axis_index("row")
    single = lax.dynamic_slice_in_dim(single_all, col_place * tok_col, tok_col)
    row_single = lax.dynamic_slice_in_dim(single_all, row_place * row_dev, row_dev)
    row_terms = jnp.dot(
        row_single, single_to_pair[:, :channels], preferred_element_type=jnp.float32
    )
    col_terms = jnp.dot(single, single_to_pair[:, channels:], preferred_element_type=jnp.float32)
    col_mask = (
        col_place * tok_col + jnp.arange(tok_col, dtype=jnp.int32) < valid_tokens[0]
    ).astype(jnp.float32)[:, None]

    def pair_row(operands):
        row_in, row_add = operands
        paired = (row_in.astype(jnp.float32) + row_add[None, :] + col_terms).astype(jnp.bfloat16)
        normed_row = normalize(paired, pair_gains[0]).astype(jnp.bfloat16)
        gate_up = jnp.dot(normed_row, trans_in, preferred_element_type=jnp.float32)
        inner = (jax.nn.silu(gate_up[:, : 4 * channels]) * gate_up[:, 4 * channels :]).astype(
            jnp.bfloat16
        )
        paired = (
            paired.astype(jnp.float32)
            + jnp.dot(inner, trans_out, preferred_element_type=jnp.float32)
        ).astype(jnp.bfloat16)
        normed_row = normalize(paired, pair_gains[1]).astype(jnp.bfloat16)
        tri_proj = jnp.dot(normed_row, tri_in, preferred_element_type=jnp.float32)
        left_row = (
            jax.nn.sigmoid(tri_proj[:, :channels]) * tri_proj[:, channels : 2 * channels] * col_mask
        ).astype(jnp.bfloat16)
        right_row = (
            jax.nn.sigmoid(tri_proj[:, 2 * channels : 3 * channels])
            * tri_proj[:, 3 * channels :]
            * col_mask
        ).astype(jnp.bfloat16)
        return (left_row, right_row)

    left_ops, right_ops = lax.map(pair_row, (pair_in, row_terms))
    partial_value = jnp.einsum(
        "ikc,jkc->ijc",
        left_ops,
        lax.all_gather(right_ops, "row", axis=0, tiled=True),
        preferred_element_type=jnp.float32,
    )
    summed = lax.psum_scatter(partial_value, "col", scatter_dimension=1, tiled=True)
    normed_out = normalize(summed, pair_gains[2]).astype(jnp.bfloat16)
    update = jnp.dot(normed_out.reshape(-1, channels), tri_out, preferred_element_type=jnp.float32)
    update = update.reshape(summed.shape).astype(jnp.bfloat16)
    return (single, update)


def solution(mesh):
    in_specs = (
        P(("row", "col"), None),
        P(None, ("row", "col"), None),
        P(),
        P(),
        P("row", "col", None),
        P(),
        P(),
        P(),
        P(),
        P(),
        P(),
        P(),
        P(),
        P(),
        P(),
    )
    out_specs = (P("col", None), P("row", "col", None))
    return jax.shard_map(body, mesh=mesh, in_specs=in_specs, out_specs=out_specs, check_vma=False)
```

profile of v0, /device:TPU:0, one launch (start us, length us, event | category | flops | bytes accessed | tf_op | source)
XLA Modules:
  0.0 658.5 jit_solution(9790463930272878575)
XLA Ops:
  10.2 4.8 collective-permute-start
  15.1 1.3 collective-permute-start.1
  23.1 1.2 convolution_bitcast_fusion.1
  25.4 1.8 dynamic_update_slice.10
  27.2 1.4 slice.138
  28.7 135.9 %all-reduce.2.cloned.1.call-done = f32[1280,384]{1,0:T(8,128)} async-done(((f32[1280,384]{1,0:T(8,128)}), f32[1280,384]{1,0:T(8,128)}) %all-reduce.2.cloned.1.call-update) | async-done | bytes 1966096 | tf_op jit(solution)/shard_map/psum | solution.py:112
  164.6 1.8 divide_convert_fusion
  166.4 1.2 fusion.46
  167.6 1.6 fusion.48
  169.3 184.3 %while.13 = (s32[]{:T(128)}, bf16[32,320,128]{2,1,0:T(8,128)(2,1)}, bf16[32,320,128]{2,1,0:T(8,128)(2,1)S(1)}, bf16[32,320,128]{2,1,0:T(8,128)(2,1)}, f32[32,128...) while((s32[]{:T(128)}, bf16[32,320,128]{2,1,0:T(8,128)(2,1)}, ...), condition=%wide.region_13.14_spmd.clone, body=%wide.region_8.13_spmd.clone.sunk | while | flops 170354240 | bytes 5716877 | solution.py:151
  170.1 1.0 convert_reduce_fusion.4
  171.7 1.3 fusion.127
  177.5 1.3 fusion.127
  181.6 1.0 convert_reduce_fusion.4
  183.3 1.3 fusion.127
  187.3 1.0 convert_reduce_fusion.4
  189.0 1.3 fusion.127
  194.8 1.3 fusion.127
  198.9 1.0 convert_reduce_fusion.4
  200.5 1.3 fusion.127
  204.6 1.0 convert_reduce_fusion.4
  206.3 1.3 fusion.127
  210.4 1.0 convert_reduce_fusion.4
  212.0 1.3 fusion.127
  216.1 1.0 convert_reduce_fusion.4
  217.8 1.3 fusion.127
  221.9 1.0 convert_reduce_fusion.4
  223.6 1.3 fusion.127
  227.6 1.0 convert_reduce_fusion.4
  229.3 1.3 fusion.127
  233.4 1.0 convert_reduce_fusion.4
  235.1 1.3 fusion.127
  239.1 1.0 convert_reduce_fusion.4
  240.8 1.3 fusion.127
  244.9 1.0 convert_reduce_fusion.4
  246.6 1.3 fusion.127
  252.3 1.3 fusion.127
  256.4 1.0 convert_reduce_fusion.4
  258.1 1.3 fusion.127
  263.9 1.3 fusion.127
  269.6 1.3 fusion.127
  275.4 1.3 fusion.127
  281.2 1.3 fusion.127
  286.9 1.3 fusion.127
  292.7 1.3 fusion.127
  298.4 1.3 fusion.127
  304.2 1.3 fusion.127
  310.0 1.3 fusion.127
  315.7 1.3 fusion.127
  321.5 1.3 fusion.127
  327.2 1.3 fusion.127
  333.0 1.3 fusion.127
  338.8 1.3 fusion.127
  344.5 1.3 fusion.127
  350.3 1.3 fusion.127
  353.6 3.4 copy.46
  357.1 3.8 copy.47
  361.0 215.0 %all-gather.2.cloned.1.call-done = bf16[256,320,128]{1,0,2:T(8,128)(2,1)} async-done(((bf16[32,320,128]{1,0,2:T(8,128)(2,1)}), bf16[256,320,128]{1,0,2:T(8,128)(2,1)}) %all-gather.2.cloned.1.call-update) | async-done | bytes 20971536 | tf_op jit(solution)/shard_map/all_gather | solution.py:155
  575.9 13.8 %convolution_bitcast_fusion = f32[32,256,128]{1,0,2:T(8,128)} fusion(bf16[256,320,128]{1,0,2:T(8,128)(2,1)} %all-gather.2.cloned.1.call-done, bf16[32,320,128]{1,0,2:T(8,128)(2,1)S(1)} %copy.47), kind=kOutput, calls=%fused_computation.54 | convolution fusion | flops 671088640 | bytes 27787264 | tf_op jit(solution)/shard_map/ikc,jkc->ijc/dot_general | solution.py:152
  589.7 6.0 copy.48
  596.4 50.3 %reduce-scatter.2.cloned.1.call-done = f32[32,64,128]{2,0,1:T(8,128)} async-done(((f32[32,256,128]{2,0,1:T(8,128)}), f32[32,64,128]{2,0,1:T(8,128)}) %reduce-scatter.2.cloned.1.call-update) | async-done | bytes 1048592 | tf_op jit(solution)/shard_map/reduce_scatter | solution.py:158
  646.7 1.7 reduce_sum.94
  648.4 1.9 multiply_reduce_fusion.1
  650.9 1.1 convolution_convert_fusion
  (442 shorter events, 138.1 us)
Async XLA Ops:
  7.2 2.0 copy-start
  7.2 15.2 %copy-start.6 = (f32[4,160,128]{2,1,0:T(8,128)S(1)}, f32[4,160,128]{2,1,0:T(8,128)}, u32[]{:S(2)}) copy-start(f32[4,160,128]{2,1,0:T(8,128)} %param.18) | copy-start | bytes 983044
  7.2 157.4 %all-reduce.2.cloned.1.call-start = ((), (), s32[]{:S(2)}) async-start(), calls=%async_computation.1 | async-start | bytes 3932160 | tf_op jit(solution)/shard_map/psum | solution.py:112
  10.2 11.8 %collective-permute-start = (bf16[48,256]{1,0:T(8,128)(2,1)S(1)}, bf16[48,256]{1,0:T(8,128)(2,1)S(1)}, u32[]{:S(2)}, u32[]{:S(2)}) collective-permute-start(bf16[48,256]{1,0:T(8,128)(2,1)S(1)} %get-tuple-element.126), channel_id=1, source_target_pairs={{0,1},{1,2},{2,3},{3,4},{4,5},{5,6},{6,7},{7,8},{8,9},{9,10},{10,1... | collective-permute-start | bytes 73736 | tf_op jit(solution)/shard_map/ppermute | solution.py:19
  15.1 7.0 %collective-permute-start.1 = (bf16[48,256]{1,0:T(8,128)(2,1)S(1)}, bf16[48,256]{1,0:T(8,128)(2,1)S(1)}, u32[]{:S(2)}, u32[]{:S(2)}) collective-permute-start(bf16[48,256]{1,0:T(8,128)(2,1)S(1)} %get-tuple-element.125), channel_id=1, source_target_pairs={{1,0},{2,1},{3,2},{4,3},{5,4},{6,5},{7,6},{8,7},{9,8},{10,9},{11,1... | collective-permute-start | bytes 73736 | tf_op jit(solution)/shard_map/ppermute | solution.py:20
  22.1 2.5 copy-start.5
  22.2 2.5 copy-start.7
  22.2 2.5 copy-start.8
  28.6 140.7 %copy-start.2 = (bf16[128,1024]{1,0:T(8,128)(2,1)S(1)}, bf16[128,1024]{1,0:T(8,128)(2,1)}, u32[]{:S(2)}) copy-start(bf16[128,1024]{1,0:T(8,128)(2,1)} %param.28) | copy-start | bytes 786436
  28.6 140.7 %copy-start.3 = (bf16[128,512]{1,0:T(8,128)(2,1)S(1)}, bf16[128,512]{1,0:T(8,128)(2,1)}, u32[]{:S(2)}) copy-start(bf16[128,512]{1,0:T(8,128)(2,1)} %param.30) | copy-start | bytes 393220
  28.6 547.3 %all-gather.2.cloned.1.call-start = ((), (), s32[]{:S(2)}) async-start(), calls=%async_computation.2 | async-start | bytes 28311552 | tf_op jit(solution)/shard_map/all_gather | solution.py:155
  166.4 2.9 copy-start.4
  357.1 289.6 %reduce-scatter.2.cloned.1.call-start = ((), (), s32[]{:S(2)}) async-start(), calls=%async_computation.3 | async-start | bytes 5242880 | tf_op jit(solution)/shard_map/reduce_scatter | solution.py:158
  595.7 55.2 %copy-start.9 = (bf16[128,128]{1,0:T(8,128)(2,1)S(1)}, bf16[128,128]{1,0:T(8,128)(2,1)}, u32[]{:S(2)}) copy-start(bf16[128,128]{1,0:T(8,128)(2,1)} %param.31) | copy-start | bytes 98308
  646.7 3.6 copy-start.1
Sparse Core Ops, SparseCore 0:
  28.7 135.7 all-reduce.1
  357.2 218.6 all-gather.1
  595.8 50.8 reduce-scatter.1
where the time goes:
time: 663 us; the launch traced here: 659 us
  waiting for transfers between devices  401 us (60%)
  other arithmetic  106 us (16%)
  matrix products  85.3 us (13%)
  local copies, waits for them, and re-layouts  43.3 us (7%)
  between operations  16.1 us (2%)
    all_gather x1, waiting for transfers between devices, body(): lax.all_gather(right_ops, 'row', axis=0, tiled=True)  215 us
    psum x1, waiting for transfers between devices, body(): totals = lax.psum(table_sums, ('row', 'col'))  136 us
    reduce_scatter x1, waiting for transfers between devices, body(): lax.psum_scatter(partial_value, 'col', scatter_dimension=1, tiled=True)  50.3 us
    dot_general x32, matrix products, pair_row(): jnp.dot(inner, trans_out, preferred_element_type=jnp.float32)  42.2 us
    reduce_sum x34, other arithmetic, normalize(): average = jnp.mean(values, axis=-1, keepdims=True)  35.6 us
    mul x33, local copies, waits for them, and re-layouts, normalize(): return centered * lax.rsqrt(variance + EPS) * gain_row  25.1 us
    dynamic_update_slice x32, other arithmetic, body(): left_ops, right_ops = lax.map(pair_row, (pair_in, row_terms))  24.9 us
    convert_element_type x32, other arithmetic, body(): col_mask = (col_place * tok_col + jnp.arange(tok_col, dtype=jnp.int32) <...  21.4 us
  transfers between devices with their start and end apart: 5, of which 3 were waited for; matrix products, arithmetic and copies ran while one was open for 1% of the time, Pallas kernels for 0%

commit v1 on v0

--- a/solution.py
+++ b/solution.py
@@ -109,7 +109,7 @@
     table_sums = jnp.zeros((tokens + atom_rows, hidden.shape[1]), jnp.float32)
     table_sums = lax.dynamic_update_slice_in_dim(table_sums, window, first_token, 0)[:tokens]
     count_float = atom_counts.astype(jnp.float32)
-    totals = lax.psum(table_sums, ("row", "col"))
+    totals = jnp.sum(lax.all_gather(table_sums, ("row", "col")), axis=0)
     single_all = (totals / count_float[:, None]).astype(jnp.bfloat16)
     row_dev, tok_col, channels = pair_in.shape
     col_place = lax.axis_index("col")

time: 663 us -> 828 us (1.25)
  waiting for transfers between devices: 401 us -> 604 us
  matrix products: 85.3 us -> 53.9 us
  local copies, waits for them, and re-layouts: 43.3 us -> 21 us
  other arithmetic: 106 us -> 124 us
    all_gather x0 -> x1, waiting for transfers between devices: none -> 339 us  [body(): totals = jnp.sum(lax.all_gather(table_sums, ('row', 'col')), axis=0)]
    psum x1 -> x0, waiting for transfers between devices: 136 us -> none  [body(): totals = lax.psum(table_sums, ('row', 'col'))]
    dot_general x32, matrix products: 42.2 us -> 13.3 us  [pair_row(): jnp.dot(inner, trans_out, preferred_element_type=jnp.float32)]
    mul x33, local copies, waits for them, and re-layouts: 25.1 us -> 0.24 us  [normalize(): return centered * lax.rsqrt(variance + EPS) * gain_row]
    reduce_sum x0 -> x1, other arithmetic: none -> 19.8 us  [body(): totals = jnp.sum(lax.all_gather(table_sums, ('row', 'col')), axis=0)]
where the time goes in v1:
time: 828 us; the launch traced here: 826 us
  waiting for transfers between devices  604 us (73%)
  other arithmetic  124 us (15%)
  matrix products  53.9 us (7%)
  local copies, waits for them, and re-layouts  21 us (3%)
  between operations  16.2 us (2%)
    all_gather x1, waiting for transfers between devices, body(): totals = jnp.sum(lax.all_gather(table_sums, ('row', 'col')), axis=0)  339 us
    all_gather x1, waiting for transfers between devices, body(): lax.all_gather(right_ops, 'row', axis=0, tiled=True)  214 us
    reduce_scatter x1, waiting for transfers between devices, body(): lax.psum_scatter(partial_value, 'col', scatter_dimension=1, tiled=True)  51 us
    reduce_sum x34, other arithmetic, normalize(): average = jnp.mean(values, axis=-1, keepdims=True)  35.6 us
    dynamic_update_slice x32, other arithmetic, body(): left_ops, right_ops = lax.map(pair_row, (pair_in, row_terms))  25.1 us
    convert_element_type x32, other arithmetic, body(): col_mask = (col_place * tok_col + jnp.arange(tok_col, dtype=jnp.int32) <...  21.4 us
    reduce_sum x1, other arithmetic, body(): totals = jnp.sum(lax.all_gather(table_sums, ('row', 'col')), axis=0)  19.8 us
    reduce_sum x66, other arithmetic, normalize(): variance = jnp.mean(centered * centered, axis=-1, keepdims=True)  17.2 us
  transfers between devices with their start and end apart: 5, of which 3 were waited for; matrix products, arithmetic and copies ran while one was open for 1% of the time, Pallas kernels for 0%

profile of v1, /device:TPU:0, one launch (start us, length us, event | category | flops | bytes accessed | tf_op | source)
XLA Modules:
  0.0 826.2 jit_solution(17797780901890282111)
XLA Ops:
  7.2 0.9 convert_reduce_fusion.2
  8.2 1.0 fusion.52
  9.2 1.0 fusion.95
  10.2 4.8 collective-permute-start
  15.1 1.3 collective-permute-start.1
  16.4 1.0 reduce-window.9
  17.6 0.8 fusion.94
  23.1 1.2 convolution_bitcast_fusion.1
  25.4 1.8 dynamic_update_slice.10
  27.2 1.4 slice.138
  28.7 338.7 %all-gather.6.cloned.1.call-done = f32[40960,384]{1,0:T(8,128)} async-done(((f32[1280,384]{1,0:T(8,128)}), f32[40960,384]{1,0:T(8,128)}) %all-gather.6.cloned.1.call-update) | async-done | bytes 62914576 | tf_op jit(solution)/shard_map/all_gather | solution.py:112
  367.4 19.8 %reduce_sum.103 = f32[1280,384]{1,0:T(8,128)S(1)} reduce(f32[32,1280,384]{2,1,0:T(8,128)} %bitcast.78, f32[]{:T(128)} %constant.35.clone.1), dimensions={0}, to_apply=%region_7.8 | reduce | flops 15237120 | bytes 64880644 | tf_op jit(solution)/shard_map/reduce_sum | solution.py:112
  388.9 131.5 %while.13 = (s32[]{:T(128)}, bf16[32,320,128]{2,1,0:T(8,128)(2,1)}, bf16[32,320,128]{2,1,0:T(8,128)(2,1)}, bf16[32,320,128]{2,1,0:T(8,128)(2,1)}, f32[32,128]{1,...) while((s32[]{:T(128)}, bf16[32,320,128]{2,1,0:T(8,128)(2,1)}, ...), condition=%wide.region_13.14_spmd.clone, body=%wide.region_8.13_spmd.clone.sunk | while | flops 170354240 | bytes 5716109 | solution.py:151
  388.9 1.0 convert_reduce_fusion.4
  392.2 0.8 bitcast_dynamic-update-slice_fusion.3
  393.0 1.0 convert_reduce_fusion.4
  397.1 1.0 convert_reduce_fusion.4
  401.2 1.0 convert_reduce_fusion.4
  405.3 1.0 convert_reduce_fusion.4
  409.4 1.0 convert_reduce_fusion.4
  413.5 1.0 convert_reduce_fusion.4
  416.8 0.8 bitcast_dynamic-update-slice_fusion.3
  417.6 1.0 convert_reduce_fusion.4
  421.7 1.0 convert_reduce_fusion.4
  425.8 1.0 convert_reduce_fusion.4
  429.9 1.0 convert_reduce_fusion.4
  433.3 0.8 bitcast_dynamic-update-slice_fusion.3
  434.1 1.0 convert_reduce_fusion.4
  438.2 1.0 convert_reduce_fusion.4
  441.5 0.8 bitcast_dynamic-update-slice_fusion.3
  442.3 1.0 convert_reduce_fusion.4
  445.6 0.8 bitcast_dynamic-update-slice_fusion.3
  446.4 1.0 convert_reduce_fusion.4
  450.5 1.0 convert_reduce_fusion.4
  454.7 1.0 convert_reduce_fusion.4
  458.8 1.0 convert_reduce_fusion.4
  462.1 0.8 bitcast_dynamic-update-slice_fusion.3
  462.9 1.0 convert_reduce_fusion.4
  467.0 1.0 convert_reduce_fusion.4
  470.3 0.8 bitcast_dynamic-update-slice_fusion.3
  471.1 1.0 convert_reduce_fusion.4
  475.2 1.0 convert_reduce_fusion.4
  479.3 1.0 convert_reduce_fusion.4
  482.6 0.8 bitcast_dynamic-update-slice_fusion.3
  483.4 1.0 convert_reduce_fusion.4
  486.7 0.8 bitcast_dynamic-update-slice_fusion.3
  487.5 1.0 convert_reduce_fusion.4
  490.9 0.8 bitcast_dynamic-update-slice_fusion.3
  491.7 1.0 convert_reduce_fusion.4
  495.8 1.0 convert_reduce_fusion.4
  499.8 1.0 convert_reduce_fusion.4
  503.9 1.0 convert_reduce_fusion.4
  508.0 1.0 convert_reduce_fusion.4
  512.1 1.0 convert_reduce_fusion.4
  516.3 1.0 convert_reduce_fusion.4
  520.4 5.0 copy.46
  525.4 3.8 copy.47
  529.2 214.3 %all-gather.4.cloned.1.call-done = bf16[256,320,128]{1,0,2:T(8,128)(2,1)} async-done(((bf16[32,320,128]{1,0,2:T(8,128)(2,1)}), bf16[256,320,128]{1,0,2:T(8,128)(2,1)}) %all-gather.4.cloned.1.call-update) | async-done | bytes 20971536 | tf_op jit(solution)/shard_map/all_gather | solution.py:155
  743.6 13.8 %convolution_bitcast_fusion = f32[32,256,128]{1,0,2:T(8,128)} fusion(bf16[256,320,128]{1,0,2:T(8,128)(2,1)} %all-gather.4.cloned.1.call-done, bf16[32,320,128]{1,0,2:T(8,128)(2,1)S(1)} %copy.47), kind=kOutput, calls=%fused_computation.54 | convolution fusion | flops 671088640 | bytes 27787264 | tf_op jit(solution)/shard_map/ikc,jkc->ijc/dot_general | solution.py:152
  757.3 6.0 copy.48
  763.4 51.0 %reduce-scatter.2.cloned.1.call-done = f32[32,64,128]{2,0,1:T(8,128)} async-done(((f32[32,256,128]{2,0,1:T(8,128)}), f32[32,64,128]{2,0,1:T(8,128)}) %reduce-scatter.2.cloned.1.call-update) | async-done | bytes 1048592 | tf_op jit(solution)/shard_map/reduce_scatter | solution.py:158
  814.4 1.7 reduce_sum.104
  816.0 1.9 multiply_reduce_fusion.1
  818.6 1.1 convolution_convert_fusion
  (451 shorter events, 95.9 us)
Async XLA Ops:
  7.2 2.0 copy-start
  7.2 15.3 %copy-start.7 = (f32[4,160,128]{2,1,0:T(8,128)S(1)}, f32[4,160,128]{2,1,0:T(8,128)}, u32[]{:S(2)}) copy-start(f32[4,160,128]{2,1,0:T(8,128)} %param.18) | copy-start | bytes 983044
  7.2 360.2 %all-gather.6.cloned.1.call-start = ((), (), s32[]{:S(2)}) async-start(), calls=%async_computation.3 | async-start | bytes 64880640 | tf_op jit(solution)/shard_map/all_gather | solution.py:112
  10.2 11.8 %collective-permute-start = (bf16[48,256]{1,0:T(8,128)(2,1)S(1)}, bf16[48,256]{1,0:T(8,128)(2,1)S(1)}, u32[]{:S(2)}, u32[]{:S(2)}) collective-permute-start(bf16[48,256]{1,0:T(8,128)(2,1)S(1)} %get-tuple-element.126), channel_id=1, source_target_pairs={{0,1},{1,2},{2,3},{3,4},{4,5},{5,6},{6,7},{7,8},{8,9},{9,10},{10,1... | collective-permute-start | bytes 73736 | tf_op jit(solution)/shard_map/ppermute | solution.py:19
  15.1 7.0 collective-permute-start.1
  22.1 2.5 copy-start.6
  22.2 2.5 copy-start.9
  22.2 2.5 copy-start.10
  28.7 714.9 %all-gather.4.cloned.1.call-start = ((), (), s32[]{:S(2)}) async-start(), calls=%async_computation.1 | async-start | bytes 28311552 | tf_op jit(solution)/shard_map/all_gather | solution.py:155
  387.3 0.9 copy-start.8
  387.3 1.3 copy-start.3
  387.3 1.3 copy-start.4
  387.3 1.3 copy-start.12
  387.3 1.3 copy-start.13
  388.2 0.7 copy-start.5
  525.4 289.0 %reduce-scatter.2.cloned.1.call-start = ((), (), s32[]{:S(2)}) async-start(), calls=%async_computation.2 | async-start | bytes 5242880 | tf_op jit(solution)/shard_map/reduce_scatter | solution.py:158
  763.3 55.2 %copy-start.11 = (bf16[128,128]{1,0:T(8,128)(2,1)S(1)}, bf16[128,128]{1,0:T(8,128)(2,1)}, u32[]{:S(2)}) copy-start(bf16[128,128]{1,0:T(8,128)(2,1)} %param.31) | copy-start | bytes 98308
  763.3 56.3 %copy-start.1 = (bf16[128,512]{1,0:T(8,128)(2,1)S(1)}, bf16[128,512]{1,0:T(8,128)(2,1)}, u32[]{:S(2)}) copy-start(bf16[128,512]{1,0:T(8,128)(2,1)} %param.23) | copy-start | bytes 393220
  814.4 3.6 copy-start.2
Sparse Core Ops, SparseCore 0:
  28.8 338.5 all-gather.5
  525.5 218.0 all-gather.3
  763.4 50.8 reduce-scatter.1
